TPU v7x, 256 devices: a whole 4x4x8 slice. The times are simulated.
256 devices in a mesh: dp: 8 (over z), ctx: 32 (over x, y, core).
Axes of the slice: x: 4, y: 4, z: 8, core: 2. Of those that a mesh axis runs over, the one named last changes fastest.
Arguments:
- head_inputs: bfloat16 [8, 4096, 2048], P('dp', 'ctx'), may hold values from -11 to 11
- entry_operator: bfloat16 [8, 4096, 128], P('dp', 'ctx'), may hold values from -3 to 3
- memory_readout: bfloat16 [8, 4096, 128], P('dp', 'ctx'), may hold values from -0.1796875 to 0.1796875
- unshifted_strides: float32 [8, 64, 4096], P('dp', None, 'ctx'), may hold values from -1.5 to 5.5, as said below
- log_decay_rates: float32 [64], P('dp'), may hold values from -11 to -2
- stride_shift: float32 [64], P('dp'), may hold values from -0.5 to 0.5
- bypass_coefficients: float32 [64], P('dp'), may hold values from 0.5 to 1.5
- result_cotangent: bfloat16 [8, 4096, 2048], P('dp', 'ctx'), may hold values from -26 to 26
Outputs:
- output: bfloat16 [8, 4096, 2048], P('dp', 'ctx')
- channels_grad: bfloat16 [8, 4096, 2048], P('dp', 'ctx')
- input_map_grad: float32 [8, 4096, 128], P('dp', 'ctx')
- output_map_grad: float32 [8, 4096, 128], P('dp', 'ctx')
- timestep_raw_gradient: float32 [8, 64, 4096], P('dp', None, 'ctx')
- a_log_grad: float32 [64], P('dp')
- bias_grad: float32 [64], P('dp')
- skip_grad: float32 [64], P('dp')
Inputs may be any that keep to these rules, and one draw needn't show every extreme that they name: `unshifted_strides`: step sizes are moderate at most positions, with a few large ones in each sequence.
All inputs are finite; a program needn't handle non-finite values.
Results may differ from a plain program's by a relative error of at most 0.001.
Values sent between devices are 32-bit elements; how exact they have to be, the bound alone decides.
A program may use at most 128 MiB of HBM per device.

v0:
```python
import jax
import jax.numpy as jnp
from jax import lax
from jax.sharding import Mesh
from jax.sharding import PartitionSpec as P

CTX = ("ctx_0", "ctx_1", "ctx_2")
maximal_accuracy = lax.Precision.HIGHEST


def rows_first(arrays, axis, dims):
    turned = [jnp.moveaxis(a, dim, 0) for a, dim in zip(arrays, dims)]
    widths = [t[0].size for t in turned]
    both = jnp.concatenate([t.reshape(-1, w) for t, w in zip(turned, widths)], axis=1)
    result = lax.all_gather(both, axis, axis=0, tiled=True)
    tiles = jnp.split(result, [sum(widths[:k]) for k in range(1, len(widths))], axis=1)
    return tuple(
        (
            jnp.moveaxis(b.reshape(-1, *t.shape[1:]), 0, dim)
            for b, t, dim in zip(tiles, turned, dims)
        )
    )


def nothing_yet(array, identity):
    return jax.tree.map(
        lambda a, e: jnp.broadcast_to(jnp.asarray(e, a.dtype), a.shape), array, identity
    )


def entering(array, axes, combine, identity, reverse):
    before = start = nothing_yet(array, identity)
    subtotal = array
    for axis in reversed(axes):
        devices, position = (lax.axis_size(axis), lax.axis_index(axis))
        pieces = jax.tree.map(lambda part: lax.all_gather(part, axis), subtotal)
        inside, subtotal = (start, start)
        for k in reversed(range(devices)) if reverse else range(devices):
            passed = k > position if reverse else k < position
            subtotal = combine(subtotal, jax.tree.map(lambda part: part[k], pieces))
            inside = jax.tree.map(lambda new, old: jnp.where(passed, new, old), subtotal, inside)
        before = combine(inside, before)
    return before


def split_up(array, dim, devices):
    dims = array.shape
    tiles = array.reshape(*dims[:dim], devices, dims[dim] // devices, *dims[dim + 1 :])
    return jnp.moveaxis(tiles, dim, 0)


def summed_on_arrival(array, axis, dim):
    devices = lax.axis_size(axis)
    tiles = lax.all_to_all(split_up(array, dim, devices), axis, 0, 0, tiled=True)
    return jnp.sum(tiles, axis=0)


def copy_for_each(array, axis):
    devices = lax.axis_size(axis)
    return lax.all_to_all(
        jnp.broadcast_to(array[None], (devices, *array.shape)), axis, 0, 0, tiled=True
    )


def of_everyone(array, axis):
    everything = copy_for_each(array, axis)
    return jnp.sum(everything, axis=0)


def packed_total(arrays, axis):
    vector, at, gathered = (jnp.concatenate([a.reshape(-1) for a in arrays]), 0, [])
    subtotal = of_everyone(vector, axis)
    for a in arrays:
        gathered.append(subtotal[at : at + a.size].reshape(a.shape))
        at += a.size
    return tuple(gathered)


def local_part(xg, write_operator, gram, dtr, rate_log, bias, skip):
    count = xg.shape[0]
    heads = dtr.shape[0]
    xg3 = xg.reshape(count, heads, -1)
    step = jax.nn.softplus(dtr + bias[:, None])
    logdecay = -jnp.exp(rate_log)[:, None] * step
    cum = jnp.cumsum(logdecay, axis=1)
    rows = lax.broadcasted_iota(jnp.int32, (count, count), 0)
    cols = lax.broadcasted_iota(jnp.int32, (count, count), 1)
    diff = cum[:, :, None] - cum[:, None, :]
    seg = jnp.exp(jnp.where((rows >= cols)[None], diff, -jnp.inf))
    weights = gram[None] * seg * step[:, None, :]
    inner = jnp.einsum("hts,shp->thp", weights, xg3, precision=maximal_accuracy)
    y_part = inner + skip[None, :, None] * xg3
    tail = jnp.exp(cum[:, -1:] - cum) * step
    scaled = xg3 * tail.T[:, :, None]
    state = jnp.einsum("shp,sn->hpn", scaled, write_operator, precision=maximal_accuracy)
    return (y_part, state, jnp.exp(cum))


def combine(earlier, later):
    return (earlier[0] * later[0], later[0][:, None, None] * earlier[1] + later[1])


def local(
    head_inputs,
    entry_operator,
    memory_readout,
    unshifted_strides,
    log_decay_rates,
    stride_shift,
    bypass_coefficients,
    result_cotangent,
):
    rate_all, full_bias_vector, skip_all = rows_first(
        (log_decay_rates, stride_shift, bypass_coefficients), "dp", (0, 0, 0)
    )
    tokens = head_inputs[0].astype(jnp.float32)
    write_operator = entry_operator[0].astype(jnp.float32)
    cmat = memory_readout[0].astype(jnp.float32)
    gram = lax.dot_general(
        memory_readout[0],
        entry_operator[0],
        (((1,), (1,)), ((), ())),
        preferred_element_type=jnp.float32,
    )
    raw = unshifted_strides[0]
    upstream = result_cotangent[0].astype(jnp.float32)
    heads = raw.shape[0]
    width = tokens.shape[1] // heads
    count = tokens.shape[0]
    parts = 1
    per = heads // parts
    output_pieces, dx_list, dt_list, rate_list, bias_list, skip_list = ([], [], [], [], [], [])
    cmat_grad = jnp.zeros_like(cmat)
    (y_part, state, growth_factor), backward = jax.vjp(
        local_part, tokens, write_operator, gram, raw, rate_all, full_bias_vector, skip_all
    )
    ends = growth_factor[:, -1]
    identity = (jnp.ones_like(ends), jnp.zeros_like(state))
    _, carried = entering((ends, state), CTX, combine, identity, False)
    readout = jnp.einsum("tn,hpn->thp", cmat, carried, precision=maximal_accuracy)
    output_pieces.append(y_part + growth_factor.T[:, :, None] * readout)
    g_group = upstream.reshape(count, per, width)
    dread = growth_factor.T[:, :, None] * g_group
    growth_grad = jnp.einsum("thp,thp->ht", g_group, readout, precision=maximal_accuracy)
    local_grad = jnp.einsum("thp,tn->hpn", dread, cmat, precision=maximal_accuracy)
    cmat_grad = cmat_grad + jnp.einsum("thp,hpn->tn", dread, carried, precision=maximal_accuracy)
    _, later = entering((ends, local_grad), CTX, combine, identity, True)
    end_grad = jnp.sum(later * carried, axis=(1, 2))
    growth_grad = growth_grad.at[:, -1].add(end_grad)
    grads = backward((g_group, later, growth_grad))
    dx_list.append(grads[0])
    bmat_grad = grads[1]
    gram_grad = grads[2]
    dt_list.append(grads[3])
    rate_list.append(grads[4])
    bias_list.append(grads[5])
    skip_list.append(grads[6])
    cmat_grad = cmat_grad + jnp.dot(gram_grad, write_operator, precision=maximal_accuracy)
    bmat_grad = bmat_grad + jnp.dot(gram_grad.T, cmat, precision=maximal_accuracy)
    core = output_pieces[0].reshape(count, heads * width)
    channels_grad = dx_list[0]
    timestep_raw_gradient = dt_list[0]
    rate_grad = rate_list[0]
    bias_grad = bias_list[0]
    skip_grad = skip_list[0]
    shares = (
        summed_on_arrival(rate_grad, "dp", 0),
        summed_on_arrival(bias_grad, "dp", 0),
        summed_on_arrival(skip_grad, "dp", 0),
    )
    owned = packed_total((shares[0], shares[1], shares[2]), CTX)
    return (
        core.astype(jnp.bfloat16)[None],
        channels_grad.astype(jnp.bfloat16)[None],
        bmat_grad[None],
        cmat_grad[None],
        timestep_raw_gradient[None],
        owned[0],
        owned[1],
        owned[2],
    )


def solution(mesh):
    torus = Mesh(mesh.devices.reshape(mesh.shape["dp"], 4, 4, 2), ("dp", "ctx_0", "ctx_1", "ctx_2"))
    return jax.shard_map(
        local,
        mesh=torus,
        in_specs=(
            P("dp", CTX, None),
            P("dp", CTX, None),
            P("dp", CTX, None),
            P("dp", None, CTX),
            P("dp"),
            P("dp"),
            P("dp"),
            P("dp", CTX, None),
        ),
        out_specs=(
            P("dp", CTX, None),
            P("dp", CTX, None),
            P("dp", CTX, None),
            P("dp", CTX, None),
            P("dp", None, CTX),
            P("dp"),
            P("dp"),
            P("dp"),
        ),
        check_vma=False,
    )
```

profile of v0, /device:TPU:1, one launch (start us, length us, event | category | flops | bytes accessed | tf_op | source)
XLA Modules:
  0.0 376.4 jit_solution(17329192003138858828)
XLA Ops:
  7.9 20.4 %all-gather.4 = f32[8,8,3]{1,2,0:T(4,128)S(1)} all-gather(f32[1,8,3]{1,2,0:T(4,128)S(1)} %maximum_bitcast_fusion), channel_id=1, replica_groups=mesh['dp'=8,'ctx_0'=4,'ctx_1'=4,'ctx_2'=2] {'dp'}, dimensions={0}, use_global_device_ids=true | all-gather | bytes 864 | tf_op jit(solution)/shard_map/all_gather | solution.py:15
  40.8 8.6 %all-reduce.1 = f32[128]{0:T(128)S(1)} all-reduce(f32[128]{0:T(128)S(1)} %dynamic-update-slice.3), channel_id=2, replica_groups=mesh['dp'=8,'ctx_0'=4,'ctx_1'=4,'ctx_2'=2] {'ctx_2'}, use_global_device_ids=true, to_apply=%add.1 | all-reduce | flops 128 | bytes 1024
  49.5 7.6 %all-gather.24.cloned.1.call-done = f32[128,32,128]{2,1,0:T(8,128)} async-done(((f32[64,32,128]{2,1,0:T(8,128)}), f32[128,32,128]{2,1,0:T(8,128)}) %all-gather.24.cloned.1.call-update) | async-done | bytes 2097168 | tf_op jit(solution)/shard_map/all_gather | solution.py:36
  60.0 8.2 %all-reduce.2 = f32[256]{0:T(256)S(1)} all-reduce(f32[256]{0:T(256)S(1)} %get-tuple-element.107), channel_id=5, replica_groups=mesh['dp'=8,'ctx_0'=4,'ctx_1'=4,'ctx_2'=2] {'ctx_1'}, use_global_device_ids=true, to_apply=%add.2 | all-reduce | flops 256 | bytes 2048
  68.3 7.8 %all-gather.22.cloned.1.call-done = f32[128,32,128]{2,1,0:T(8,128)} async-done(((f32[64,32,128]{2,1,0:T(8,128)}), f32[128,32,128]{2,1,0:T(8,128)}) %all-gather.22.cloned.1.call-update) | async-done | bytes 2097168 | tf_op jit(solution)/shard_map/all_gather | solution.py:36
  78.9 50.5 %all-gather.18.cloned.1.call-done = f32[4,64,32,128]{3,2,1,0:T(8,128)} async-done(((f32[1,64,32,128]{3,2,1,0:T(8,128)}), f32[4,64,32,128]{3,2,1,0:T(8,128)}) %all-gather.18.cloned.1.call-update) | async-done | bytes 4194320 | tf_op jit(solution)/shard_map/all_gather | solution.py:36
  129.4 52.9 %all-gather.14.cloned.1.call-done = f32[4,64,32,128]{3,2,1,0:T(8,128)} async-done(((f32[1,64,32,128]{3,2,1,0:T(8,128)}), f32[4,64,32,128]{3,2,1,0:T(8,128)}) %all-gather.14.cloned.1.call-update) | async-done | bytes 4194320 | tf_op jit(solution)/shard_map/all_gather | solution.py:36
  182.3 4.8 %multiply_add_fusion = (f32[1,64,32,128]{3,2,1,0:T(8,128)}, f32[1,64,32,128]{3,2,1,0:T(8,128)}) fusion(f32[4,64,32,128]{3,2,1,0:T(8,128)} %all-gather.18.cloned.1.call-done, f32[64]{0:T(128)S(1)} %get-tuple-element.98, f32[64]{0:T(128)S(1)} %get-tuple-element.97, f32[64]{0:T(128)S(1)} %get-tuple-element.95, f32[64]{0:T(128)S(1)} %get-tuple-element.96, ...), kind=kLoop, calls=%fused_computation.86 | loop fusion | flops 3670016 | bytes 10487296 | tf_op jit(solution)/shard_map/add | solution.py:100
  188.5 6.7 %all-to-all-start.2 = ((f32[8,1,8]{2,1,0:T(1,128)}), f32[8,1,8]{2,1,0:T(1,128)S(1)}, u32[]{:S(2)}, u32[]{:S(2)}) async-start(f32[8,1,8]{2,1,0:T(1,128)} %bitcast.81), calls=%async_computation.2 | async-start | bytes 8192 | tf_op jit(solution)/shard_map/all_to_all | solution.py:54
  195.3 7.6 %all-gather.6 = f32[4,1,64]{2,1,0:T(1,128)S(1)} all-gather(f32[1,1,64]{2,1,0:T(1,128)S(1)} %get-tuple-element.92), channel_id=1, replica_groups=mesh['dp'=8,'ctx_0'=4,'ctx_1'=4,'ctx_2'=2] {'ctx_0'}, dimensions={0}, use_global_device_ids=true | all-gather | bytes 1280 | tf_op jit(solution)/shard_map/all_gather | solution.py:36
  202.9 6.2 %all-gather.5 = f32[4,1,64]{2,1,0:T(1,128)S(1)} all-gather(f32[1,1,64]{2,1,0:T(1,128)S(1)} %get-tuple-element.93), channel_id=1, replica_groups=mesh['dp'=8,'ctx_0'=4,'ctx_1'=4,'ctx_2'=2] {'ctx_0'}, dimensions={0}, use_global_device_ids=true | all-gather | bytes 1280 | tf_op jit(solution)/shard_map/all_gather | solution.py:36
  211.3 27.1 %all-gather.20.cloned.1.call-done = f32[4,64,32,128]{3,2,1,0:T(8,128)} async-done(((f32[1,64,32,128]{3,2,1,0:T(8,128)}), f32[4,64,32,128]{3,2,1,0:T(8,128)}) %all-gather.20.cloned.1.call-update) | async-done | bytes 4194320 | tf_op jit(solution)/shard_map/all_gather | solution.py:36
  238.4 5.0 %add_add_fusion = f32[1,64,32,128]{3,2,1,0:T(8,128)S(1)} fusion(f32[1,64,32,128]{3,2,1,0:T(8,128)} %get-tuple-element.100, f32[4,64,32,128]{3,2,1,0:T(8,128)} %all-gather.20.cloned.1.call-done, f32[4,64,32,128]{3,2,1,0:T(8,128)} %all-gather.18.cloned.1.call-done, f32[128,32,128]{2,1,0:T(8,128)} %all-gather.24.cloned.1.call-done, ...), kind=kLoop, calls=%fused_computation.85 | loop fusion | flops 7602176 | bytes 11537162 | tf_op jit(solution)/shard_map/add | solution.py:100
  246.3 45.0 %all-gather.16.cloned.1.call-done = f32[4,64,32,128]{3,2,1,0:T(8,128)} async-done(((f32[1,64,32,128]{3,2,1,0:T(8,128)}), f32[4,64,32,128]{3,2,1,0:T(8,128)}) %all-gather.16.cloned.1.call-update) | async-done | bytes 4194320 | tf_op jit(solution)/shard_map/all_gather | solution.py:36
  291.3 8.6 %fusion.50 = f32[64]{0:T(128)S(1)} fusion(f32[4,64,32,128]{3,2,1,0:T(8,128)} %all-gather.20.cloned.1.call-done, f32[4,64,32,128]{3,2,1,0:T(8,128)} %all-gather.18.cloned.1.call-done, f32[128,32,128]{2,1,0:T(8,128)} %all-gather.24.cloned.1.call-done, f32[4,64,32,128]{3,2,1,0:T(8,128)} %all-gather.16.cloned.1.call-done, ...), kind=kLoop, calls=%fused_computation.49 | loop fusion | flops 16777152 | bytes 20977428 | tf_op jit(solution)/shard_map/reduce_sum | solution.py:148
  305.6 4.4 %add_add_fusion.1 = f32[1,64,32,128]{3,2,1,0:T(8,128)S(1)} fusion(f32[1,64,32,128]{3,2,1,0:T(8,128)} %get-tuple-element.101, f32[4,64,32,128]{3,2,1,0:T(8,128)} %all-gather.16.cloned.1.call-done, f32[4,64,32,128]{3,2,1,0:T(8,128)} %all-gather.14.cloned.1.call-done, f32[128,32,128]{2,1,0:T(8,128)S(1)} %copy-done.1, f32[64]{0:T(128)S(1)} %get-tuple-element.71, ...), kind=kLoop, calls=%fused_computation.89 | loop fusion | flops 7602176 | bytes 11537162 | tf_op jit(solution)/shard_map/add | solution.py:100
  313.0 4.9 %fusion.7 = (f32[64,128]{1,0:T(8,128)S(1)}, f32[64,128]{1,0:T(8,128)S(1)}, f32[64,128]{1,0:T(8,128)S(1)}, f32[128,128]{1,0:T(8,128)S(1)}) fusion(f32[64,128]{1,0:T(8,128)} %get-tuple-element.76, f32[64,128]{1,0:T(8,128)S(1)} %reduce_window_sum.22, f32[128,128]{1,0:T(8,128)} %fusion.78, pred[128,128]{1,0:T(8,128)(4,1)} %iota_compare_fusion, ...), kind=kOutput, calls=%fused_computation.9 | convolution fusion | flops 80699392 | bytes 1359872 | tf_op jit(solution)/shard_map/transpose(jvp(hts,shp->thp))/dot_general | solution.py:91
  320.8 6.7 %all-to-all-start.1 = ((f32[8,1,8]{2,1,0:T(1,128)}), f32[8,1,8]{2,1,0:T(1,128)S(1)}, u32[]{:S(2)}, u32[]{:S(2)}) async-start(f32[8,1,8]{2,1,0:T(1,128)} %bitcast.80), calls=%async_computation.1 | async-start | bytes 8192 | tf_op jit(solution)/shard_map/all_to_all | solution.py:54
  327.6 5.7 %fusion.38 = bf16[128,64,32]{0,2,1:T(8,128)(2,1)S(1)} fusion(bf16[128,64,32]{0,2,1:T(8,128)(2,1)S(1)} %bitcast.326, f32[64,128]{1,0:T(8,128)} %get-tuple-element.76, f32[64,128]{1,0:T(8,128)S(1)} %reduce_window_sum.22, f32[128,128]{1,0:T(8,128)} %fusion.78, pred[128,128]{1,0:T(8,128)(4,1)} %iota_compare_fusion, f32[64,32,128]{2,1,0:T(8,128)} %get-tuple-element.113, ...), kind=kOutput, calls=%fused_computation.34 | convolution fusion | flops 408420352 | bytes 2277632 | tf_op jit(solution)/shard_map/jvp(hts,shp->thp)/dot_general | solution.py:91
  333.4 3.5 fusion.35
  339.5 6.6 %all-to-all-start = ((f32[8,1,8]{2,1,0:T(1,128)}), f32[8,1,8]{2,1,0:T(1,128)S(1)}, u32[]{:S(2)}, u32[]{:S(2)}) async-start(f32[8,1,8]{2,1,0:T(1,128)} %bitcast.79), calls=%async_computation | async-start | bytes 8192 | tf_op jit(solution)/shard_map/all_to_all | solution.py:54
  347.0 5.6 %all-to-all-done = f32[8,1,8]{2,1,0:T(1,128)S(1)} async-done(((f32[8,1,8]{2,1,0:T(1,128)}), f32[8,1,8]{2,1,0:T(1,128)S(1)}, u32[]{:S(2)}, u32[]{:S(2)}) %all-to-all-start) | async-done | bytes 288 | tf_op jit(solution)/shard_map/all_to_all | solution.py:54
  353.3 8.6 %all-to-all-start.3 = ((f32[32,1,24]{2,1,0:T(1,128)}), f32[32,1,24]{2,1,0:T(1,128)S(1)}, u32[]{:S(2)}, u32[]{:S(2)}) async-start(f32[32,1,24]{2,1,0:T(1,128)} %broadcast_in_dim.71), calls=%async_computation.3 | async-start | bytes 32768 | tf_op jit(solution)/shard_map/all_to_all | solution.py:60
  364.8 4.0 %all-to-all-done.3 = f32[32,1,24]{2,1,0:T(1,128)S(1)} async-done(((f32[32,1,24]{2,1,0:T(1,128)}), f32[32,1,24]{2,1,0:T(1,128)S(1)}, u32[]{:S(2)}, u32[]{:S(2)}) %all-to-all-start.3) | async-done | bytes 3104 | tf_op jit(solution)/shard_map/all_to_all | solution.py:60
  (126 shorter events, 43.4 us)
Async XLA Ops:
  7.2 29.0 %copy-start = (bf16[1,128,128]{2,1,0:T(8,128)(2,1)S(1)}, bf16[1,128,128]{2,1,0:T(8,128)(2,1)}, u32[]{:S(2)}) copy-start(bf16[1,128,128]{2,1,0:T(8,128)(2,1)} %param.11) | copy-start | bytes 98308
  7.2 27.3 %copy-start.13 = (bf16[1,128,128]{2,1,0:T(8,128)(2,1)S(1)}, bf16[1,128,128]{2,1,0:T(8,128)(2,1)}, u32[]{:S(2)}) copy-start(bf16[1,128,128]{2,1,0:T(8,128)(2,1)} %param.12) | copy-start | bytes 98308
  7.2 49.9 %all-gather.24.cloned.1.call-start = ((), (), s32[]{:S(2)}) async-start(), calls=%async_computation.9 | async-start | bytes 3145728 | tf_op jit(solution)/shard_map/all_gather | solution.py:36
  34.4 25.5 %copy-start.2 = (f32[1,128,2048]{1,2,0:T(8,128)}, f32[1,128,2048]{1,2,0:T(8,128)S(1)}, u32[]{:S(2)}) copy-start(f32[1,128,2048]{1,2,0:T(8,128)S(1)} %get-tuple-element.74) | copy-start | bytes 3145732
  36.1 40.0 %all-gather.22.cloned.1.call-start = ((), (), s32[]{:S(2)}) async-start(), calls=%async_computation.8 | async-start | bytes 3145728 | tf_op jit(solution)/shard_map/all_gather | solution.py:36
  37.8 91.6 %all-gather.18.cloned.1.call-start = ((), (), s32[]{:S(2)}) async-start(), calls=%async_computation.6 | async-start | bytes 5242880 | tf_op jit(solution)/shard_map/all_gather | solution.py:36
  59.9 122.4 %all-gather.14.cloned.1.call-start = ((), (), s32[]{:S(2)}) async-start(), calls=%async_computation.4 | async-start | bytes 5242880 | tf_op jit(solution)/shard_map/all_gather | solution.py:36
  78.9 159.5 %all-gather.20.cloned.1.call-start = ((), (), s32[]{:S(2)}) async-start(), calls=%async_computation.7 | async-start | bytes 5242880 | tf_op jit(solution)/shard_map/all_gather | solution.py:36
  187.1 104.2 %all-gather.16.cloned.1.call-start = ((), (), s32[]{:S(2)}) async-start(), calls=%async_computation.5 | async-start | bytes 5242880 | tf_op jit(solution)/shard_map/all_gather | solution.py:36
  188.5 22.1 %all-to-all-start.2 = ((f32[8,1,8]{2,1,0:T(1,128)}), f32[8,1,8]{2,1,0:T(1,128)S(1)}, u32[]{:S(2)}, u32[]{:S(2)}) async-start(f32[8,1,8]{2,1,0:T(1,128)} %bitcast.81), calls=%async_computation.2 | async-start | bytes 8192 | tf_op jit(solution)/shard_map/all_to_all | solution.py:54
  209.7 81.6 %copy-start.19 = (f32[64]{0:T(128)}, f32[64]{0:T(128)S(1)}, u32[]{:S(2)}) copy-start(f32[64]{0:T(128)S(1)} %get-tuple-element.89) | copy-start | bytes 772
  209.7 81.6 %copy-start.20 = (f32[64]{0:T(128)}, f32[64]{0:T(128)S(1)}, u32[]{:S(2)}) copy-start(f32[64]{0:T(128)S(1)} %get-tuple-element.90) | copy-start | bytes 772
  209.7 81.6 %copy-start.21 = (f32[64]{0:T(128)}, f32[64]{0:T(128)S(1)}, u32[]{:S(2)}) copy-start(f32[64]{0:T(128)S(1)} %get-tuple-element.91) | copy-start | bytes 772
  238.4 6.0 %copy-start.3 = (f32[1,128,2048]{1,2,0:T(8,128)S(1)}, f32[1,128,2048]{1,2,0:T(8,128)}, u32[]{:S(2)}) copy-start(f32[1,128,2048]{1,2,0:T(8,128)} %copy-done.2) | copy-start | bytes 3145732
  238.4 52.9 %copy-start.1 = (f32[128,32,128]{2,1,0:T(8,128)S(1)}, f32[128,32,128]{2,1,0:T(8,128)}, u32[]{:S(2)}) copy-start(f32[128,32,128]{2,1,0:T(8,128)} %all-gather.22.cloned.1.call-done) | copy-start | bytes 6291460
  291.3 11.7 %copy-start.14 = (f32[1,64,128]{2,1,0:T(8,128)S(1)}, f32[1,64,128]{2,1,0:T(8,128)}, u32[]{:S(2)}) copy-start(f32[1,64,128]{2,1,0:T(8,128)} %param.13) | copy-start | bytes 98308
  313.0 14.5 %copy-start.11 = (bf16[1,128,2048]{1,2,0:T(8,128)(2,1)S(1)}, bf16[1,128,2048]{1,2,0:T(8,128)(2,1)}, u32[]{:S(2)}) copy-start(bf16[1,128,2048]{1,2,0:T(8,128)(2,1)} %copy-done.10) | copy-start | bytes 1572868
  320.8 18.7 %all-to-all-start.1 = ((f32[8,1,8]{2,1,0:T(1,128)}), f32[8,1,8]{2,1,0:T(1,128)S(1)}, u32[]{:S(2)}, u32[]{:S(2)}) async-start(f32[8,1,8]{2,1,0:T(1,128)} %bitcast.80), calls=%async_computation.1 | async-start | bytes 8192 | tf_op jit(solution)/shard_map/all_to_all | solution.py:54
  327.5 5.8 %copy-start.9 = (bf16[1,128,2048]{1,2,0:T(8,128)(2,1)S(1)}, bf16[1,128,2048]{1,2,0:T(8,128)(2,1)}, u32[]{:S(2)}) copy-start(bf16[1,128,2048]{1,2,0:T(8,128)(2,1)} %copy-done.7) | copy-start | bytes 1572868
  327.5 5.8 %copy-start.12 = (f32[128,64,32]{0,2,1:T(8,128)S(1)}, f32[128,64,32]{0,2,1:T(8,128)}, u32[]{:S(2)}) copy-start(f32[128,64,32]{0,2,1:T(8,128)} %get-tuple-element.111) | copy-start | bytes 3145732
  327.5 5.8 %copy-start.16 = (f32[128,128]{1,0:T(8,128)S(1)}, f32[128,128]{1,0:T(8,128)}, u32[]{:S(2)}) copy-start(f32[128,128]{1,0:T(8,128)} %fusion.78) | copy-start | bytes 196612
  333.4 19.2 %copy-start.22 = (f32[8]{0:T(128)S(1)}, f32[8]{0:T(128)}, u32[]{:S(2)}) copy-start(f32[8]{0:T(128)} %reduce_sum.179) | copy-start | bytes 100
  339.5 13.1 %all-to-all-start = ((f32[8,1,8]{2,1,0:T(1,128)}), f32[8,1,8]{2,1,0:T(1,128)S(1)}, u32[]{:S(2)}, u32[]{:S(2)}) async-start(f32[8,1,8]{2,1,0:T(1,128)} %bitcast.79), calls=%async_computation | async-start | bytes 8192 | tf_op jit(solution)/shard_map/all_to_all | solution.py:54
  353.3 15.6 %all-to-all-start.3 = ((f32[32,1,24]{2,1,0:T(1,128)}), f32[32,1,24]{2,1,0:T(1,128)S(1)}, u32[]{:S(2)}, u32[]{:S(2)}) async-start(f32[32,1,24]{2,1,0:T(1,128)} %broadcast_in_dim.71), calls=%async_computation.3 | async-start | bytes 32768 | tf_op jit(solution)/shard_map/all_to_all | solution.py:60
  (12 other events, 50.6 us)
Sparse Core Ops, SparseCore 0:
  36.2 20.8 all-gather.23
  58.9 17.1 all-gather.21
  77.9 51.4 all-gather.17
  131.1 51.1 all-gather.13
  187.2 51.1 all-gather.19
  240.1 51.1 all-gather.15
where the time goes:
time: 377 us; the launch traced here: 376 us
  waiting for transfers between devices  201 us (53%)
  blocking collectives  50.9 us (14%)
  other arithmetic  37.9 us (10%)
  starting transfers between devices  29 us (8%)
  matrix products  28.2 us (7%)
  between operations  15.9 us (4%)
  local copies, waits for them, and re-layouts  13.2 us (4%)
    all_gather x6, waiting for transfers between devices, entering(): pieces = jax.tree.map(lambda part: lax.all_gather(part, axis), subtotal)  191 us
    all_gather x1, blocking collectives, rows_first(): result = lax.all_gather(both, axis, axis=0, tiled=True)  20.4 us
    all_to_all x3, starting transfers between devices, summed_on_arrival(): lax.all_to_all(split_up(array, dim, devices), axis, 0, 0, tiled=True)  20.1 us
    add x5, other arithmetic, combine(): later[0][:, None, None] * earlier[1] + later[1]  19.6 us
    unnamed x2, blocking collectives  16.7 us
    dot_general x3, matrix products, local_part(): inner = jnp.einsum('hts,shp->thp', weights, xg3, precision=maximal_accuracy)  14.2 us
    all_gather x2, blocking collectives, entering(): pieces = jax.tree.map(lambda part: lax.all_gather(part, axis), subtotal)  13.7 us
    all_to_all x1, starting transfers between devices, copy_for_each(): lax.all_to_all(jnp.broadcast_to(array[None], (devices, *array.shape)), ax...  8.61 us
  transfers between devices with their start and end apart: 10, of which 8 were waited for; matrix products, arithmetic and copies ran while one was open for 9% of the time, Pallas kernels for 0%

commit v1 on v0

--- a/solution.py
+++ b/solution.py
@@ -12,7 +12,10 @@
     turned = [jnp.moveaxis(a, dim, 0) for a, dim in zip(arrays, dims)]
     widths = [t[0].size for t in turned]
     both = jnp.concatenate([t.reshape(-1, w) for t, w in zip(turned, widths)], axis=1)
-    result = lax.all_gather(both, axis, axis=0, tiled=True)
+    devices_2 = lax.axis_size(axis)
+    blocks = jnp.stack([both for _ in range(devices_2)])
+    blocks = lax.all_to_all(blocks, axis, split_axis=0, concat_axis=0)
+    result = jnp.concatenate(blocks, axis=0)
     tiles = jnp.split(result, [sum(widths[:k]) for k in range(1, len(widths))], axis=1)
     return tuple(
         (

time: 377 us -> 364 us (0.966)
  blocking collectives: 50.9 us -> 26.1 us
  starting transfers between devices: 29 us -> 38 us
    all_gather x1 -> x0, blocking collectives: 20.4 us -> none  [rows_first(): result = lax.all_gather(both, axis, axis=0, tiled=True)]
    all_to_all x0 -> x1, starting transfers between devices: none -> 9.01 us  [rows_first(): blocks = lax.all_to_all(blocks, axis, split_axis=0, concat_axis=0)]
    unnamed x2, blocking collectives: 16.7 us -> 12.4 us
    unnamed x62 -> x61, local copies, waits for them, and re-layouts: 8.43 us -> 8.32 us
  transfers between devices with their start and end apart: 10 -> 11, of which waited for: 8 -> 9; matrix products, arithmetic and copies ran while one was open for 9% -> 10% of each run, Pallas kernels for 0% -> 0%
where the time goes in v1:
time: 364 us; the launch traced here: 363 us
  waiting for transfers between devices  203 us (56%)
  starting transfers between devices  38 us (10%)
  other arithmetic  37.8 us (10%)
  matrix products  28.2 us (8%)
  blocking collectives  26.1 us (7%)
  between operations  15.9 us (4%)
  local copies, waits for them, and re-layouts  13.8 us (4%)
    all_gather x6, waiting for transfers between devices, entering(): pieces = jax.tree.map(lambda part: lax.all_gather(part, axis), subtotal)  189 us
    all_to_all x3, starting transfers between devices, summed_on_arrival(): lax.all_to_all(split_up(array, dim, devices), axis, 0, 0, tiled=True)  20.1 us
    add x5, other arithmetic, combine(): later[0][:, None, None] * earlier[1] + later[1]  19.6 us
    dot_general x3, matrix products, local_part(): inner = jnp.einsum('hts,shp->thp', weights, xg3, precision=maximal_accuracy)  14.2 us
    all_gather x2, blocking collectives, entering(): pieces = jax.tree.map(lambda part: lax.all_gather(part, axis), subtotal)  13.7 us
    unnamed x2, blocking collectives  12.4 us
    all_to_all x1, starting transfers between devices, rows_first(): blocks = lax.all_to_all(blocks, axis, split_axis=0, concat_axis=0)  9.01 us
    all_to_all x1, starting transfers between devices, copy_for_each(): lax.all_to_all(jnp.broadcast_to(array[None], (devices, *array.shape)), ax...  8.61 us
  transfers between devices with their start and end apart: 11, of which 9 were waited for; matrix products, arithmetic and copies ran while one was open for 10% of the time, Pallas kernels for 0%

profile of v1, /device:TPU:1, one launch (start us, length us, event | category | flops | bytes accessed | tf_op | source)
XLA Modules:
  0.0 363.3 jit_solution(9746469955427785559)
XLA Ops:
  8.5 9.0 %all-to-all-start = ((f32[8,8,3]{1,2,0:T(4,128)}), f32[8,8,3]{1,2,0:T(4,128)S(1)}, u32[]{:S(2)}, u32[]{:S(2)}) async-start(f32[8,8,3]{1,2,0:T(4,128)} %stack.2), calls=%async_computation | async-start | bytes 32768 | tf_op jit(solution)/shard_map/all_to_all | solution.py:17
  20.4 3.7 %all-to-all-done = f32[8,8,3]{1,2,0:T(4,128)S(1)} async-done(((f32[8,8,3]{1,2,0:T(4,128)}), f32[8,8,3]{1,2,0:T(4,128)S(1)}, u32[]{:S(2)}, u32[]{:S(2)}) %all-to-all-start) | async-done | bytes 800 | tf_op jit(solution)/shard_map/all_to_all | solution.py:17
  33.7 4.2 %all-reduce.1 = f32[128]{0:T(128)S(1)} all-reduce(f32[128]{0:T(128)S(1)} %dynamic-update-slice.3), channel_id=2, replica_groups=mesh['dp'=8,'ctx_0'=4,'ctx_1'=4,'ctx_2'=2] {'ctx_2'}, use_global_device_ids=true, to_apply=%add.1 | all-reduce | flops 128 | bytes 1024
  38.0 6.1 %all-gather.23.cloned.1.call-done = f32[128,32,128]{2,1,0:T(8,128)} async-done(((f32[64,32,128]{2,1,0:T(8,128)}), f32[128,32,128]{2,1,0:T(8,128)}) %all-gather.23.cloned.1.call-update) | async-done | bytes 2097168 | tf_op jit(solution)/shard_map/all_gather | solution.py:39
  47.0 8.2 %all-reduce.2 = f32[256]{0:T(256)S(1)} all-reduce(f32[256]{0:T(256)S(1)} %get-tuple-element.115), channel_id=5, replica_groups=mesh['dp'=8,'ctx_0'=4,'ctx_1'=4,'ctx_2'=2] {'ctx_1'}, use_global_device_ids=true, to_apply=%add.2 | all-reduce | flops 256 | bytes 2048
  55.3 7.9 %all-gather.21.cloned.1.call-done = f32[128,32,128]{2,1,0:T(8,128)} async-done(((f32[64,32,128]{2,1,0:T(8,128)}), f32[128,32,128]{2,1,0:T(8,128)}) %all-gather.21.cloned.1.call-update) | async-done | bytes 2097168 | tf_op jit(solution)/shard_map/all_gather | solution.py:39
  65.9 50.5 %all-gather.17.cloned.1.call-done = f32[4,64,32,128]{3,2,1,0:T(8,128)} async-done(((f32[1,64,32,128]{3,2,1,0:T(8,128)}), f32[4,64,32,128]{3,2,1,0:T(8,128)}) %all-gather.17.cloned.1.call-update) | async-done | bytes 4194320 | tf_op jit(solution)/shard_map/all_gather | solution.py:39
  116.4 52.9 %all-gather.13.cloned.1.call-done = f32[4,64,32,128]{3,2,1,0:T(8,128)} async-done(((f32[1,64,32,128]{3,2,1,0:T(8,128)}), f32[4,64,32,128]{3,2,1,0:T(8,128)}) %all-gather.13.cloned.1.call-update) | async-done | bytes 4194320 | tf_op jit(solution)/shard_map/all_gather | solution.py:39
  169.3 4.7 %multiply_add_fusion = (f32[1,64,32,128]{3,2,1,0:T(8,128)}, f32[1,64,32,128]{3,2,1,0:T(8,128)}) fusion(f32[4,64,32,128]{3,2,1,0:T(8,128)} %all-gather.17.cloned.1.call-done, f32[64]{0:T(128)S(1)} %get-tuple-element.106, f32[64]{0:T(128)S(1)} %get-tuple-element.105, f32[64]{0:T(128)S(1)} %get-tuple-element.103, f32[64]{0:T(128)S(1)} %get-tuple-element.104, ...), kind=kLoop, calls=%fused_computation.86 | loop fusion | flops 3670016 | bytes 10487296 | tf_op jit(solution)/shard_map/add | solution.py:103
  176.9 6.7 %all-to-all-start.3 = ((f32[8,1,8]{2,1,0:T(1,128)}), f32[8,1,8]{2,1,0:T(1,128)S(1)}, u32[]{:S(2)}, u32[]{:S(2)}) async-start(f32[8,1,8]{2,1,0:T(1,128)} %bitcast.80), calls=%async_computation.3 | async-start | bytes 8192 | tf_op jit(solution)/shard_map/all_to_all | solution.py:57
  183.7 7.6 %all-gather.5 = f32[4,1,64]{2,1,0:T(1,128)S(1)} all-gather(f32[1,1,64]{2,1,0:T(1,128)S(1)} %get-tuple-element.100), channel_id=1, replica_groups=mesh['dp'=8,'ctx_0'=4,'ctx_1'=4,'ctx_2'=2] {'ctx_0'}, dimensions={0}, use_global_device_ids=true | all-gather | bytes 1280 | tf_op jit(solution)/shard_map/all_gather | solution.py:39
  191.3 6.2 %all-gather.4 = f32[4,1,64]{2,1,0:T(1,128)S(1)} all-gather(f32[1,1,64]{2,1,0:T(1,128)S(1)} %get-tuple-element.101), channel_id=1, replica_groups=mesh['dp'=8,'ctx_0'=4,'ctx_1'=4,'ctx_2'=2] {'ctx_0'}, dimensions={0}, use_global_device_ids=true | all-gather | bytes 1280 | tf_op jit(solution)/shard_map/all_gather | solution.py:39
  198.2 27.2 %all-gather.19.cloned.1.call-done = f32[4,64,32,128]{3,2,1,0:T(8,128)} async-done(((f32[1,64,32,128]{3,2,1,0:T(8,128)}), f32[4,64,32,128]{3,2,1,0:T(8,128)}) %all-gather.19.cloned.1.call-update) | async-done | bytes 4194320 | tf_op jit(solution)/shard_map/all_gather | solution.py:39
  225.4 5.0 %add_add_fusion = f32[1,64,32,128]{3,2,1,0:T(8,128)S(1)} fusion(f32[1,64,32,128]{3,2,1,0:T(8,128)} %get-tuple-element.108, f32[4,64,32,128]{3,2,1,0:T(8,128)} %all-gather.19.cloned.1.call-done, f32[4,64,32,128]{3,2,1,0:T(8,128)} %all-gather.17.cloned.1.call-done, f32[128,32,128]{2,1,0:T(8,128)} %all-gather.23.cloned.1.call-done, ...), kind=kLoop, calls=%fused_computation.85 | loop fusion | flops 7602176 | bytes 11537162 | tf_op jit(solution)/shard_map/add | solution.py:103
  233.2 45.0 %all-gather.15.cloned.1.call-done = f32[4,64,32,128]{3,2,1,0:T(8,128)} async-done(((f32[1,64,32,128]{3,2,1,0:T(8,128)}), f32[4,64,32,128]{3,2,1,0:T(8,128)}) %all-gather.15.cloned.1.call-update) | async-done | bytes 4194320 | tf_op jit(solution)/shard_map/all_gather | solution.py:39
  278.3 8.6 %fusion.50 = f32[64]{0:T(128)S(1)} fusion(f32[4,64,32,128]{3,2,1,0:T(8,128)} %all-gather.19.cloned.1.call-done, f32[4,64,32,128]{3,2,1,0:T(8,128)} %all-gather.17.cloned.1.call-done, f32[128,32,128]{2,1,0:T(8,128)} %all-gather.23.cloned.1.call-done, f32[4,64,32,128]{3,2,1,0:T(8,128)} %all-gather.15.cloned.1.call-done, ...), kind=kLoop, calls=%fused_computation.49 | loop fusion | flops 16777152 | bytes 20977428 | tf_op jit(solution)/shard_map/reduce_sum | solution.py:151
  292.6 4.4 %add_add_fusion.1 = f32[1,64,32,128]{3,2,1,0:T(8,128)S(1)} fusion(f32[1,64,32,128]{3,2,1,0:T(8,128)} %get-tuple-element.109, f32[4,64,32,128]{3,2,1,0:T(8,128)} %all-gather.15.cloned.1.call-done, f32[4,64,32,128]{3,2,1,0:T(8,128)} %all-gather.13.cloned.1.call-done, f32[128,32,128]{2,1,0:T(8,128)S(1)} %copy-done.1, f32[64]{0:T(128)S(1)} %get-tuple-element.79, ...), kind=kLoop, calls=%fused_computation.89 | loop fusion | flops 7602176 | bytes 11537162 | tf_op jit(solution)/shard_map/add | solution.py:103
  300.0 4.9 %fusion.7 = (f32[64,128]{1,0:T(8,128)S(1)}, f32[64,128]{1,0:T(8,128)S(1)}, f32[64,128]{1,0:T(8,128)S(1)}, f32[128,128]{1,0:T(8,128)S(1)}) fusion(f32[64,128]{1,0:T(8,128)} %get-tuple-element.84, f32[64,128]{1,0:T(8,128)S(1)} %reduce_window_sum.22, f32[128,128]{1,0:T(8,128)} %fusion.78, pred[128,128]{1,0:T(8,128)(4,1)} %iota_compare_fusion, ...), kind=kOutput, calls=%fused_computation.9 | convolution fusion | flops 80699392 | bytes 1359872 | tf_op jit(solution)/shard_map/transpose(jvp(hts,shp->thp))/dot_general | solution.py:94
  307.7 6.7 %all-to-all-start.2 = ((f32[8,1,8]{2,1,0:T(1,128)}), f32[8,1,8]{2,1,0:T(1,128)S(1)}, u32[]{:S(2)}, u32[]{:S(2)}) async-start(f32[8,1,8]{2,1,0:T(1,128)} %bitcast.79), calls=%async_computation.2 | async-start | bytes 8192 | tf_op jit(solution)/shard_map/all_to_all | solution.py:57
  314.5 5.7 %fusion.38 = bf16[128,64,32]{0,2,1:T(8,128)(2,1)S(1)} fusion(bf16[128,64,32]{0,2,1:T(8,128)(2,1)S(1)} %bitcast.324, f32[64,128]{1,0:T(8,128)} %get-tuple-element.84, f32[64,128]{1,0:T(8,128)S(1)} %reduce_window_sum.22, f32[128,128]{1,0:T(8,128)} %fusion.78, pred[128,128]{1,0:T(8,128)(4,1)} %iota_compare_fusion, f32[64,32,128]{2,1,0:T(8,128)} %get-tuple-element.121, ...), kind=kOutput, calls=%fused_computation.34 | convolution fusion | flops 408420352 | bytes 2277632 | tf_op jit(solution)/shard_map/jvp(hts,shp->thp)/dot_general | solution.py:94
  326.4 6.6 %all-to-all-start.1 = ((f32[8,1,8]{2,1,0:T(1,128)}), f32[8,1,8]{2,1,0:T(1,128)S(1)}, u32[]{:S(2)}, u32[]{:S(2)}) async-start(f32[8,1,8]{2,1,0:T(1,128)} %bitcast.78), calls=%async_computation.1 | async-start | bytes 8192 | tf_op jit(solution)/shard_map/all_to_all | solution.py:57
  333.9 5.6 %all-to-all-done.1 = f32[8,1,8]{2,1,0:T(1,128)S(1)} async-done(((f32[8,1,8]{2,1,0:T(1,128)}), f32[8,1,8]{2,1,0:T(1,128)S(1)}, u32[]{:S(2)}, u32[]{:S(2)}) %all-to-all-start.1) | async-done | bytes 288 | tf_op jit(solution)/shard_map/all_to_all | solution.py:57
  340.3 8.6 %all-to-all-start.4 = ((f32[32,1,24]{2,1,0:T(1,128)}), f32[32,1,24]{2,1,0:T(1,128)S(1)}, u32[]{:S(2)}, u32[]{:S(2)}) async-start(f32[32,1,24]{2,1,0:T(1,128)} %broadcast_in_dim.71), calls=%async_computation.4 | async-start | bytes 32768 | tf_op jit(solution)/shard_map/all_to_all | solution.py:63
  351.8 4.0 %all-to-all-done.4 = f32[32,1,24]{2,1,0:T(1,128)S(1)} async-done(((f32[32,1,24]{2,1,0:T(1,128)}), f32[32,1,24]{2,1,0:T(1,128)S(1)}, u32[]{:S(2)}, u32[]{:S(2)}) %all-to-all-start.4) | async-done | bytes 3104 | tf_op jit(solution)/shard_map/all_to_all | solution.py:63
  (128 shorter events, 47.4 us)
Async XLA Ops:
  7.2 21.9 %copy-start = (bf16[1,128,128]{2,1,0:T(8,128)(2,1)S(1)}, bf16[1,128,128]{2,1,0:T(8,128)(2,1)}, u32[]{:S(2)}) copy-start(bf16[1,128,128]{2,1,0:T(8,128)(2,1)} %param.11) | copy-start | bytes 98308
  7.2 20.2 %copy-start.13 = (bf16[1,128,128]{2,1,0:T(8,128)(2,1)S(1)}, bf16[1,128,128]{2,1,0:T(8,128)(2,1)}, u32[]{:S(2)}) copy-start(bf16[1,128,128]{2,1,0:T(8,128)(2,1)} %param.12) | copy-start | bytes 98308
  8.5 15.6 %all-to-all-start = ((f32[8,8,3]{1,2,0:T(4,128)}), f32[8,8,3]{1,2,0:T(4,128)S(1)}, u32[]{:S(2)}, u32[]{:S(2)}) async-start(f32[8,8,3]{1,2,0:T(4,128)} %stack.2), calls=%async_computation | async-start | bytes 32768 | tf_op jit(solution)/shard_map/all_to_all | solution.py:17
  17.5 26.6 %all-gather.23.cloned.1.call-start = ((), (), s32[]{:S(2)}) async-start(), calls=%async_computation.10 | async-start | bytes 3145728 | tf_op jit(solution)/shard_map/all_gather | solution.py:39
  18.9 11.8 %copy-start.7 = (bf16[1,128,2048]{1,2,0:T(8,128)(2,1)}, bf16[1,128,2048]{1,2,0:T(8,128)(2,1)S(1)}, u32[]{:S(2)}) copy-start(bf16[1,128,2048]{1,2,0:T(8,128)(2,1)S(1)} %copy.80) | copy-start | bytes 1572868
  20.4 10.3 %copy-start.10 = (bf16[1,128,2048]{1,2,0:T(8,128)(2,1)}, bf16[1,128,2048]{1,2,0:T(8,128)(2,1)S(1)}, u32[]{:S(2)}) copy-start(bf16[1,128,2048]{1,2,0:T(8,128)(2,1)S(1)} %copy.78) | copy-start | bytes 1572868
  27.3 19.6 %copy-start.2 = (f32[1,128,2048]{1,2,0:T(8,128)}, f32[1,128,2048]{1,2,0:T(8,128)S(1)}, u32[]{:S(2)}) copy-start(f32[1,128,2048]{1,2,0:T(8,128)S(1)} %get-tuple-element.82) | copy-start | bytes 3145732
  29.0 34.1 %all-gather.21.cloned.1.call-start = ((), (), s32[]{:S(2)}) async-start(), calls=%async_computation.9 | async-start | bytes 3145728 | tf_op jit(solution)/shard_map/all_gather | solution.py:39
  30.7 85.7 %all-gather.17.cloned.1.call-start = ((), (), s32[]{:S(2)}) async-start(), calls=%async_computation.7 | async-start | bytes 5242880 | tf_op jit(solution)/shard_map/all_gather | solution.py:39
  46.9 122.4 %all-gather.13.cloned.1.call-start = ((), (), s32[]{:S(2)}) async-start(), calls=%async_computation.5 | async-start | bytes 5242880 | tf_op jit(solution)/shard_map/all_gather | solution.py:39
  65.9 159.5 %all-gather.19.cloned.1.call-start = ((), (), s32[]{:S(2)}) async-start(), calls=%async_computation.8 | async-start | bytes 5242880 | tf_op jit(solution)/shard_map/all_gather | solution.py:39
  174.1 104.2 %all-gather.15.cloned.1.call-start = ((), (), s32[]{:S(2)}) async-start(), calls=%async_computation.6 | async-start | bytes 5242880 | tf_op jit(solution)/shard_map/all_gather | solution.py:39
  176.9 20.7 %all-to-all-start.3 = ((f32[8,1,8]{2,1,0:T(1,128)}), f32[8,1,8]{2,1,0:T(1,128)S(1)}, u32[]{:S(2)}, u32[]{:S(2)}) async-start(f32[8,1,8]{2,1,0:T(1,128)} %bitcast.80), calls=%async_computation.3 | async-start | bytes 8192 | tf_op jit(solution)/shard_map/all_to_all | solution.py:57
  197.5 80.8 %copy-start.19 = (f32[64]{0:T(128)}, f32[64]{0:T(128)S(1)}, u32[]{:S(2)}) copy-start(f32[64]{0:T(128)S(1)} %get-tuple-element.97) | copy-start | bytes 772
  197.5 80.8 %copy-start.20 = (f32[64]{0:T(128)}, f32[64]{0:T(128)S(1)}, u32[]{:S(2)}) copy-start(f32[64]{0:T(128)S(1)} %get-tuple-element.98) | copy-start | bytes 772
  197.5 80.7 %copy-start.21 = (f32[64]{0:T(128)}, f32[64]{0:T(128)S(1)}, u32[]{:S(2)}) copy-start(f32[64]{0:T(128)S(1)} %get-tuple-element.99) | copy-start | bytes 772
  225.4 6.0 %copy-start.3 = (f32[1,128,2048]{1,2,0:T(8,128)S(1)}, f32[1,128,2048]{1,2,0:T(8,128)}, u32[]{:S(2)}) copy-start(f32[1,128,2048]{1,2,0:T(8,128)} %copy-done.2) | copy-start | bytes 3145732
  225.4 52.9 %copy-start.1 = (f32[128,32,128]{2,1,0:T(8,128)S(1)}, f32[128,32,128]{2,1,0:T(8,128)}, u32[]{:S(2)}) copy-start(f32[128,32,128]{2,1,0:T(8,128)} %all-gather.21.cloned.1.call-done) | copy-start | bytes 6291460
  278.2 11.7 %copy-start.14 = (f32[1,64,128]{2,1,0:T(8,128)S(1)}, f32[1,64,128]{2,1,0:T(8,128)}, u32[]{:S(2)}) copy-start(f32[1,64,128]{2,1,0:T(8,128)} %param.13) | copy-start | bytes 98308
  300.0 14.5 %copy-start.11 = (bf16[1,128,2048]{1,2,0:T(8,128)(2,1)S(1)}, bf16[1,128,2048]{1,2,0:T(8,128)(2,1)}, u32[]{:S(2)}) copy-start(bf16[1,128,2048]{1,2,0:T(8,128)(2,1)} %copy-done.10) | copy-start | bytes 1572868
  307.7 18.7 %all-to-all-start.2 = ((f32[8,1,8]{2,1,0:T(1,128)}), f32[8,1,8]{2,1,0:T(1,128)S(1)}, u32[]{:S(2)}, u32[]{:S(2)}) async-start(f32[8,1,8]{2,1,0:T(1,128)} %bitcast.79), calls=%async_computation.2 | async-start | bytes 8192 | tf_op jit(solution)/shard_map/all_to_all | solution.py:57
  320.4 19.2 %copy-start.22 = (f32[8]{0:T(128)S(1)}, f32[8]{0:T(128)}, u32[]{:S(2)}) copy-start(f32[8]{0:T(128)} %reduce_sum.179) | copy-start | bytes 100
  326.4 13.1 %all-to-all-start.1 = ((f32[8,1,8]{2,1,0:T(1,128)}), f32[8,1,8]{2,1,0:T(1,128)S(1)}, u32[]{:S(2)}, u32[]{:S(2)}) async-start(f32[8,1,8]{2,1,0:T(1,128)} %bitcast.78), calls=%async_computation.1 | async-start | bytes 8192 | tf_op jit(solution)/shard_map/all_to_all | solution.py:57
  340.3 15.6 %all-to-all-start.4 = ((f32[32,1,24]{2,1,0:T(1,128)}), f32[32,1,24]{2,1,0:T(1,128)S(1)}, u32[]{:S(2)}, u32[]{:S(2)}) async-start(f32[32,1,24]{2,1,0:T(1,128)} %broadcast_in_dim.71), calls=%async_computation.4 | async-start | bytes 32768 | tf_op jit(solution)/shard_map/all_to_all | solution.py:63
  (13 other events, 58.9 us)
Sparse Core Ops, SparseCore 0:
  29.1 14.9 all-gather.22
  45.9 17.1 all-gather.20
  65.0 51.4 all-gather.16
  118.1 51.1 all-gather.12
  174.2 51.1 all-gather.18
  227.1 51.1 all-gather.14
